TPU v7x, 32 devices: a whole 2x2x4 slice. The times are simulated.
32 devices in a mesh: group: 2 (over x), src: 16 (over z, y, core).
Axes of the slice: x: 2, y: 2, z: 4, core: 2. Of those that a mesh axis runs over, the one named last changes fastest.
Arguments:
- rcv_points: float32 [3, 4096], P(None, ('group', 'src')), parts along dimension 1, may hold values from -1 to 1
- rcv_normals: float32 [3, 4096], P(None, ('group', 'src')), parts along dimension 1, may hold values from -4 to 4
- left_modes: float32 [8, 4096], P(None, ('group', 'src')), parts along dimension 1, may hold values from -5 to 5
- vertices: float32 [3, 2048], P(None, ('group', 'src')), parts along dimension 1, may hold values from -1 to 1
- connect: int32 [2, 4096], P(None, ('group', 'src')), parts along dimension 1, may hold values from 0 to 1023, as said below
- right_modes: float32 [8, 4096], P(None, ('group', 'src')), parts along dimension 1, may hold values from -0.125 to 0.125
- mode_weights: float32 [16], P('group'), parts along dimension 0, may hold values from 0.25 to 1
Outputs:
- rcv_grad: float32 [6, 4096], P(None, ('group', 'src')), parts along dimension 1
- vert_grad: float32 [3, 2048], P(None, ('group', 'src')), parts along dimension 1
There are 2 independent parts, one for each index of `group`. A program takes and returns all parts, laid end to end along the dimension named above; each array names one. Nothing has to cross between parts.
Inputs may be any that keep to these rules, and one draw needn't show every extreme that they name: `connect`: a panel's first vertex is one of the 64 vertices held at the same index of src as the panel, and its second vertex is the next vertex number.
All inputs are finite; a program needn't handle non-finite values.
Results may differ from a plain program's by a relative error of at most 0.0003.
Values sent between devices are 32-bit elements; how exact they have to be, the bound alone decides.
No kernel may reach another device: no remote copies, remote signals or barrier semaphores. Data moves between devices by JAX's collectives and lax.ppermute only.
A program may use at most 64 MiB of HBM per device.

v0:
```python
import math
import jax
import jax.numpy as jnp
from jax import lax
from jax.sharding import PartitionSpec as P

core_term = 0.05
inverse_four_pi = 0.25 / math.pi


def shifted(value, axis, steps):
    count = lax.axis_size(axis)
    leading, last = (max(0, -steps), min(count, count - steps))
    return lax.ppermute(value, axis, [(source, source + steps) for source in range(leading, last)])


def lift_points(raw):
    return jnp.stack([raw[0], raw[1], 0.5 + 0.2 * raw[2]])


def place_points(raw):
    return jnp.stack([raw[0], raw[1], 0.2 * raw[2]])


def tile_energy(points, normals, first_end, second_end, coefficient):
    rel_first = points[:, None, :] - first_end[:, :, None]
    rel_second = points[:, None, :] - second_end[:, :, None]
    segment = (second_end - first_end)[:, :, None]
    cross_x = rel_first[1] * rel_second[2] - rel_first[2] * rel_second[1]
    cross_y = rel_first[2] * rel_second[0] - rel_first[0] * rel_second[2]
    cross_z = rel_first[0] * rel_second[1] - rel_first[1] * rel_second[0]
    cross_sq = cross_x * cross_x + cross_y * cross_y + cross_z * cross_z
    dist_first = jnp.sqrt(jnp.sum(rel_first * rel_first, axis=0))
    dist_second = jnp.sqrt(jnp.sum(rel_second * rel_second, axis=0))
    along_term = jnp.sum(segment * (rel_first / dist_first - rel_second / dist_second), axis=0)
    span_sq = jnp.sum(segment * segment, axis=0)
    denominator = cross_sq + core_term * (span_sq + 1.0)
    normal_term = (
        normals[0][None, :] * cross_x
        + normals[1][None, :] * cross_y
        + normals[2][None, :] * cross_z
    )
    influence = inverse_four_pi * normal_term * along_term / denominator
    return jnp.sum(coefficient * influence)


def tile_gradients(points, normals, first_end, second_end, coefficient):
    return jax.grad(tile_energy, argnums=(0, 1, 2, 3))(
        points, normals, first_end, second_end, coefficient
    )


def on_device(rcv_points, rcv_normals, left_modes, vertices, connect, right_modes, mode_weights):
    own_count = vertices.shape[1]
    next_first = shifted(vertices[:, :1], "src", -1)
    extended = jnp.concatenate([vertices, next_first], axis=1)
    places = place_points(extended)
    base_vertex = lax.axis_index("src") * own_count
    local_first = connect[0] - base_vertex
    local_second = local_first + 1
    first_end = places[:, local_first]
    second_end = places[:, local_second]
    points = lift_points(rcv_points)
    chain_scale = jnp.array([1.0, 1.0, 0.2], dtype=jnp.float32)[:, None]
    weighted = right_modes * mode_weights[:, None]
    receiver_count = rcv_points.shape[1] * lax.axis_size("src")
    source_count = connect.shape[1]
    start_totals = (
        jnp.zeros((3, source_count), jnp.float32),
        jnp.zeros((3, source_count), jnp.float32),
        jnp.zeros((6, receiver_count), jnp.float32),
    )
    shard_points = lax.all_gather(points, "src", axis=1, tiled=True)
    shard_normals = lax.all_gather(rcv_normals, "src", axis=1, tiled=True)
    shard_left = lax.all_gather(left_modes, "src", axis=1, tiled=True)
    row_count = shard_points.shape[1]
    width_rows = math.gcd(row_count, 2048)

    def advance(number, inner):
        sum_first, sum_second, receiver_buffer = inner
        local_start = number * width_rows
        block_points = lax.dynamic_slice_in_dim(shard_points, local_start, width_rows, 1)
        block_normals = lax.dynamic_slice_in_dim(shard_normals, local_start, width_rows, 1)
        block_left = lax.dynamic_slice_in_dim(shard_left, local_start, width_rows, 1)
        coefficient = jnp.einsum("mj,mi->ji", weighted, block_left, precision=lax.Precision.HIGHEST)
        grads = tile_gradients(block_points, block_normals, first_end, second_end, coefficient)
        rows_out = jnp.concatenate([grads[0] * chain_scale, grads[1]], axis=0)
        receiver_buffer = lax.dynamic_update_slice_in_dim(receiver_buffer, rows_out, local_start, 1)
        return (sum_first + grads[2], sum_second + grads[3], receiver_buffer)

    sum_first, sum_second, receiver_buffer = lax.fori_loop(
        0, row_count // width_rows, advance, start_totals
    )
    rcv_grad = lax.psum_scatter(receiver_buffer, "src", scatter_dimension=1, tiled=True)
    vertex_partial = jnp.zeros((3, own_count + 1), jnp.float32)
    vertex_partial = (
        vertex_partial.at[:, local_first].add(sum_first).at[:, local_second].add(sum_second)
    )
    incoming = shifted(vertex_partial[:, own_count:], "src", 1)
    own_part = vertex_partial[:, :own_count]
    own_part = jnp.concatenate([own_part[:, :1] + incoming, own_part[:, 1:]], axis=1)
    vert_grad = own_part * chain_scale
    return (rcv_grad, vert_grad)


def solution(mesh):
    in_specs = (
        P(None, ("group", "src")),
        P(None, ("group", "src")),
        P(None, ("group", "src")),
        P(None, ("group", "src")),
        P(None, ("group", "src")),
        P(None, ("group", "src")),
        P("group"),
    )
    out_specs = (P(None, ("group", "src")), P(None, ("group", "src")))
    return jax.shard_map(
        on_device, mesh=mesh, in_specs=in_specs, out_specs=out_specs, check_vma=False
    )
```

profile of v0, /device:TPU:0, one launch (start us, length us, event | category | flops | bytes accessed | tf_op | source)
XLA Modules:
  0.0 154.4 jit_solution(849035136935577808)
XLA Ops:
  7.2 1.3 collective-permute-start
  8.5 0.7 multiply_add_fusion.1
  9.2 0.7 slice.81
  9.9 23.8 %all_gather.10 = f32[3,2048]{1,0:T(4,128)S(1)} all-gather(f32[3,128]{1,0:T(4,128)S(1)} %pad_maximum_fusion.3), channel_id=1, replica_groups=mesh['group'=2,'src'=16] {'src'}, dimensions={1}, use_global_device_ids=true | all-gather | bytes 26112 | tf_op jit(solution)/shard_map/all_gather | solution.py:73
  33.7 17.7 %all_gather.9 = f32[3,2048]{1,0:T(4,128)S(1)} all-gather(f32[3,128]{1,0:T(4,128)} %param.9), channel_id=1, replica_groups=mesh['group'=2,'src'=16] {'src'}, dimensions={1}, use_global_device_ids=true | all-gather | bytes 26112 | tf_op jit(solution)/shard_map/all_gather | solution.py:74
  51.4 19.2 %all_gather.11 = f32[8,2048]{1,0:T(8,128)S(1)} all-gather(f32[8,128]{1,0:T(8,128)} %param.10), channel_id=1, replica_groups=mesh['group'=2,'src'=16] {'src'}, dimensions={1}, use_global_device_ids=true | all-gather | bytes 69632 | tf_op jit(solution)/shard_map/all_gather | solution.py:75
  70.6 0.7 fusion.24
  71.3 0.8 pad_maximum_fusion.1
  72.1 0.1 copy.26
  72.2 0.6 gather_fusion.1
  72.9 0.7 gather_fusion
  73.7 0.8 fusion.15
  74.6 0.3 multiply_divide_fusion.1
  74.9 0.3 multiply_divide_fusion.2
  75.3 1.8 %divide_multiply_fusion.1 = (f32[128,2048]{1,0:T(8,128)S(1)}, f32[128,2048]{1,0:T(8,128)S(1)}, f32[128,2048]{1,0:T(8,128)S(1)}, f32[128,2048]{1,0:T(8,128)S(1)},...) fusion(f32[128]{0:T(128)S(1)} %add_multiply_fusion.2, f32[2048]{0:T(1024)S(1)} %bitcast.136, ...), kind=kOutput, calls=%fused_computation.109 | convolution fusion | flops 31196160 | bytes 13726240 | tf_op jit(solution)/shard_map/while/body/eval_jaxpr/mj,mi->ji/dot_general | solution.py:85
  77.1 2.5 %multiply_reduce_fusion = (f32[3,128]{1,0:T(4,128)S(1)}, f32[128,2048]{1,0:T(8,128)S(1)}, f32[128,2048]{1,0:T(8,128)S(1)}, f32[128,2048]{1,0:T(8,128)S(1)}) fusion(f32[128,2048]{1,0:T(8,128)S(1)} %get-tuple-element.62, f32[128,2048]{1,0:T(8,128)S(1)} %get-tuple-element.92, f32[3,128]{1,0:T(4,128)S(1)} %bitcast.127, f32[128,2048]{1,0:T(8,128)S(1)} %get-tuple-element.94, ...), kind=kLoop, calls=%fused_computation.36 | loop fusion | flops 12582528 | bytes 8419328 | tf_op jit(solution)/shard_map/while/body/eval_jaxpr/transpose(jvp())/reduce_sum | solution.py:35
  79.6 0.2 multiply_multiply_fusion.3
  79.8 0.2 multiply_multiply_fusion.1
  80.1 0.6 fusion.28
  80.6 2.0 %multiply_bitcast_fusion.5 = (f32[1,128,2048]{2,1,0:T(8,128)}, f32[128,2048]{1,0:T(8,128)}, f32[128,2048]{1,0:T(8,128)S(1)}) fusion(f32[3,128,2048]{2,1,0:T(8,128)S(1)} %get-tuple-element.95, f32[128,2048]{1,0:T(8,128)S(1)} %get-tuple-element.67, f32[128,2048]{1,0:T(8,128)S(1)} %get-tuple-element.54, f32[2048]{0:T(1024)S(1)} %broadcast_multiply_fusion.2, ...), kind=kLoop, calls=%fused_computation.57 | loop fusion | flops 2359296 | bytes 9445376 | tf_op jit(solution)/shard_map/while/body/eval_jaxpr/transpose(jvp())/broadcast_in_dim | solution.py:31
  82.6 2.2 %multiply_bitcast_fusion.3 = (f32[1,128,2048]{2,1,0:T(8,128)S(1)}, f32[128,2048]{1,0:T(8,128)}, f32[1,128,2048]{2,1,0:T(8,128)S(1)}, f32[128,2048]{1,0:T(8,128)}...) fusion(f32[3,128,2048]{2,1,0:T(8,128)S(1)} %get-tuple-element.95, f32[128,2048]{1,0:T(8,128)S(1)} %get-tuple-element.66, ...), kind=kLoop, calls=%fused_computation.55 | loop fusion | flops 5236736 | bytes 11575296 | tf_op jit(solution)/shard_map/while/body/eval_jaxpr/transpose(jvp())/broadcast_in_dim | solution.py:30
  84.9 4.8 %multiply_bitcast_fusion.11 = (f32[1,128,2048]{2,1,0:T(8,128)S(1)}, f32[1,128,2048]{2,1,0:T(8,128)S(1)}, f32[1,128,2048]{2,1,0:T(8,128)S(1)}, f32[1,128,2048]{2,...) fusion(f32[128,2048]{1,0:T(8,128)} %get-tuple-element.56, ...), kind=kLoop, calls=%fused_computation.65 | loop fusion | flops 3145728 | bytes 18874368 | tf_op jit(solution)/shard_map/while/body/eval_jaxpr/transpose(jvp())/broadcast_in_dim | solution.py:31
  89.7 3.4 %fusion.27 = (f32[3,128]{1,0:T(4,128)S(1)}, f32[3,2048]{1,0:T(4,128)S(1)}) fusion(f32[1,128,2048]{2,1,0:T(8,128)} %get-tuple-element.88, f32[1,128,2048]{2,1,0:T(8,128)S(1)} %get-tuple-element.70, f32[1,128,2048]{2,1,0:T(8,128)} %get-tuple-element.89, f32[1,128,2048]{2,1,0:T(8,128)S(1)} %get-tuple-element.58, f32[1,128,2048]{2,1,0:T(8,128)} %get-tuple-element.90, ...), kind=kLoop, calls=%fused_computation.111 | loop fusion | flops 11003520 | bytes 9490944 | tf_op jit(solution)/shard_map/while/body/eval_jaxpr/transpose(jvp())/reduce_sum | solution.py:26
  93.1 1.9 %fusion.26 = (f32[3,128]{1,0:T(4,128)S(1)}, f32[3,2048]{1,0:T(4,128)S(1)}) fusion(f32[1,128,2048]{2,1,0:T(8,128)S(1)} %get-tuple-element.84, f32[1,128,2048]{2,1,0:T(8,128)S(1)} %get-tuple-element.85, f32[1,128,2048]{2,1,0:T(8,128)S(1)} %get-tuple-element.86, f32[1,128,2048]{2,1,0:T(8,128)S(1)} %copy-done, f32[1,128,2048]{2,1,0:T(8,128)S(1)} %get-tuple-element.73, ...), kind=kLoop, calls=%fused_computation.110 | loop fusion | flops 11789952 | bytes 9490944 | tf_op jit(solution)/shard_map/while/body/eval_jaxpr/transpose(jvp())/reduce_sum | solution.py:27
  95.0 0.1 copy.31
  95.2 1.0 scatter_custom_fusion
  96.2 1.2 scatter_fusion
  97.6 0.6 pad_maximum_fusion
  98.3 2.2 %collective-permute-start.1 = (f32[3,1]{0,1:T(1,128)S(1)}, f32[3,1]{0,1:T(1,128)S(1)}, u32[]{:S(2)}, u32[]{:S(2)}) collective-permute-start(f32[3,1]{0,1:T(1,128)S(1)} %slice.108), channel_id=1, source_target_pairs={{0,1},{1,2},{2,3},{3,4},{4,5},{5,6},{6,7},{7,8},{8,9},{9,10},{10,1... | collective-permute-start | bytes 44 | tf_op jit(solution)/shard_map/ppermute | solution.py:14
  100.6 0.7 collective-permute-done.1
  101.4 0.7 maximum_multiply_fusion
  102.1 45.5 %reduce-scatter.2.cloned.1.call-done = f32[6,128]{1,0:T(8,128)} async-done(((f32[6,2048]{1,0:T(8,128)}), f32[6,128]{1,0:T(8,128)}) %reduce-scatter.2.cloned.1.call-update) | async-done | bytes 3088 | tf_op jit(solution)/shard_map/reduce_scatter | solution.py:94
  (33 shorter events, 0.7 us)
Async XLA Ops:
  7.2 140.4 %reduce-scatter.2.cloned.1.call-start = ((), (), s32[]{:S(2)}) async-start(), calls=%async_computation.1 | async-start | bytes 69632 | tf_op jit(solution)/shard_map/reduce_scatter | solution.py:94
  7.2 64.1 %collective-permute-start = (f32[3,1]{1,0:T(4,128)}, f32[3,1]{1,0:T(4,128)S(1)}, u32[]{:S(2)}, u32[]{:S(2)}) collective-permute-start(f32[3,1]{1,0:T(4,128)} %bitcast.141), channel_id=1, source_target_pairs={{1,0},{2,1},{3,2},{4,3},{5,4},{6,5},{7,6},{8,7},{9,8},{10,9},{11,1... | collective-permute-start | bytes 44 | tf_op jit(solution)/shard_map/ppermute | solution.py:14
  74.5 0.7 copy-start.2
  74.5 0.7 copy-start.3
  89.7 3.4 %copy-start = (f32[1,128,2048]{2,1,0:T(8,128)S(1)}, f32[1,128,2048]{2,1,0:T(8,128)}, u32[]{:S(2)}) copy-start(f32[1,128,2048]{2,1,0:T(8,128)} %get-tuple-element.87) | copy-start | bytes 3145732
  93.1 4.4 %copy-start.1 = (f32[3]{0:T(128)S(1)}, f32[3]{0:T(128)}, u32[]{:S(2)}) copy-start(f32[3]{0:T(128)} %constant.34.clone) | copy-start | bytes 40
  98.3 3.1 %collective-permute-start.1 = (f32[3,1]{0,1:T(1,128)S(1)}, f32[3,1]{0,1:T(1,128)S(1)}, u32[]{:S(2)}, u32[]{:S(2)}) collective-permute-start(f32[3,1]{0,1:T(1,128)S(1)} %slice.108), channel_id=1, source_target_pairs={{0,1},{1,2},{2,3},{3,4},{4,5},{5,6},{6,7},{7,8},{8,9},{9,10},{10,1... | collective-permute-start | bytes 44 | tf_op jit(solution)/shard_map/ppermute | solution.py:14
Sparse Core Ops, SparseCore 0:
  98.4 49.1 reduce-scatter.1
where the time goes:
time: 155 us; the launch traced here: 154 us
  blocking collectives  60.7 us (39%)
  waiting for transfers between devices  46.3 us (30%)
  other arithmetic  25.1 us (16%)
  between operations  14.3 us (9%)
  starting transfers between devices  3.57 us (2%)
  local copies, waits for them, and re-layouts  2.68 us (2%)
  matrix products  1.85 us (1%)
    reduce_scatter x1, waiting for transfers between devices, on_device(): lax.psum_scatter(receiver_buffer, 'src', scatter_dimension=1, tiled=True)  45.5 us
    all_gather x1, blocking collectives, on_device(): shard_points = lax.all_gather(points, 'src', axis=1, tiled=True)  23.8 us
    all_gather x1, blocking collectives, on_device(): shard_left = lax.all_gather(left_modes, 'src', axis=1, tiled=True)  19.2 us
    all_gather x1, blocking collectives, on_device(): shard_normals = lax.all_gather(rcv_normals, 'src', axis=1, tiled=True)  17.7 us
    broadcast_in_dim x2, other arithmetic, tile_energy(): cross_z = rel_first[0] * rel_second[1] - rel_first[1] * rel_second[0]  6.79 us
    ppermute x2, starting transfers between devices, shifted(): lax.ppermute(value, axis, [(source, source + steps) for source in range(l...  3.54 us
    reduce_sum x1, other arithmetic, tile_energy(): rel_first = points[:, None, :] - first_end[:, :, None]  3.41 us
  transfers between devices with their start and end apart: 3, of which 2 were waited for; matrix products, arithmetic and copies ran while one was open for 2% of the time, Pallas kernels for 0%

commit v1 on v0

--- a/solution.py
+++ b/solution.py
@@ -71,7 +71,12 @@
         jnp.zeros((6, receiver_count), jnp.float32),
     )
     shard_points = lax.all_gather(points, "src", axis=1, tiled=True)
-    shard_normals = lax.all_gather(rcv_normals, "src", axis=1, tiled=True)
+    ring = [rcv_normals]
+    for hop in range(15):
+        ring.append(lax.ppermute(ring[-1], "src", [(dev, (dev + 1) % 16) for dev in range(16)]))
+    shard_normals = jnp.roll(
+        jnp.concatenate(ring[::-1], axis=1), (lax.axis_index("src") + 1) * ring[0].shape[1], axis=1
+    )
     shard_left = lax.all_gather(left_modes, "src", axis=1, tiled=True)
     row_count = shard_points.shape[1]
     width_rows = math.gcd(row_count, 2048)

time: 155 us -> 200 us (1.29)
  waiting for transfers between devices: 46.3 us -> 115 us
  blocking collectives: 60.7 us -> 36.9 us
    ppermute x0 -> x15, waiting for transfers between devices: none -> 67.3 us  [on_device(): lax.ppermute(ring[-1], 'src', [(dev, (dev + 1) % 16) for dev in range(16)])]
    all_gather x1 -> x0, blocking collectives: 17.7 us -> none  [on_device(): shard_normals = lax.all_gather(rcv_normals, 'src', axis=1, tiled=True)]
    all_gather x1, blocking collectives: 23.8 us -> 18.5 us  [on_device(): shard_points = lax.all_gather(points, 'src', axis=1, tiled=True)]
  transfers between devices with their start and end apart: 3 -> 18, of which waited for: 2 -> 15; matrix products, arithmetic and copies ran while one was open for 2% -> 3% of each run, Pallas kernels for 0% -> 0%
where the time goes in v1:
time: 200 us
  waiting for transfers between devices  115 us (58%)
  blocking collectives  36.9 us (18%)
  other arithmetic  25 us (12%)
  between operations  14.4 us (7%)
  starting transfers between devices  3.65 us (2%)
  local copies, waits for them, and re-layouts  3.04 us (2%)
    ppermute x15, waiting for transfers between devices, on_device(): lax.ppermute(ring[-1], 'src', [(dev, (dev + 1) % 16) for dev in range(16)])  67.3 us
    reduce_scatter x1, waiting for transfers between devices, on_device(): lax.psum_scatter(receiver_buffer, 'src', scatter_dimension=1, tiled=True)  46.9 us
    all_gather x1, blocking collectives, on_device(): shard_points = lax.all_gather(points, 'src', axis=1, tiled=True)  18.5 us
    all_gather x1, blocking collectives, on_device(): shard_left = lax.all_gather(left_modes, 'src', axis=1, tiled=True)  18.4 us
    broadcast_in_dim x2, other arithmetic, tile_energy(): cross_z = rel_first[0] * rel_second[1] - rel_first[1] * rel_second[0]  6.8 us
  transfers between devices with their start and end apart: 18, of which 15 were waited for; matrix products, arithmetic and copies ran while one was open for 3% of the time, Pallas kernels for 0%

profile of v1, /device:TPU:0, one launch (start us, length us, event | category | flops | bytes accessed | tf_op | source)
XLA Modules:
  0.0 199.9 jit_solution(11627072109845137642)
XLA Ops:
  7.7 1.3 collective-permute-start
  9.0 5.2 %collective-permute-done.1 = f32[3,128]{1,0:T(4,128)S(1)} collective-permute-done((f32[3,128]{1,0:T(4,128)}, f32[3,128]{1,0:T(4,128)S(1)}, u32[]{:S(2)}, u32[]{:S(2)}) %collective-permute-start.1) | collective-permute-done | bytes 1568 | tf_op jit(solution)/shard_map/ppermute | solution.py:76
  14.2 0.7 multiply_add_fusion.1
  14.9 5.0 %collective-permute-done.2 = f32[3,128]{1,0:T(4,128)S(1)} collective-permute-done((f32[3,128]{1,0:T(4,128)S(1)}, f32[3,128]{1,0:T(4,128)S(1)}, u32[]{:S(2)}, u32[]{:S(2)}) %collective-permute-start.2) | collective-permute-done | bytes 1568 | tf_op jit(solution)/shard_map/ppermute | solution.py:76
  20.6 5.0 %collective-permute-done.3 = f32[3,128]{1,0:T(4,128)S(1)} collective-permute-done((f32[3,128]{1,0:T(4,128)S(1)}, f32[3,128]{1,0:T(4,128)S(1)}, u32[]{:S(2)}, u32[]{:S(2)}) %collective-permute-start.3) | collective-permute-done | bytes 1568 | tf_op jit(solution)/shard_map/ppermute | solution.py:76
  25.6 0.7 slice.81
  26.3 5.0 %collective-permute-done.4 = f32[3,128]{1,0:T(4,128)S(1)} collective-permute-done((f32[3,128]{1,0:T(4,128)S(1)}, f32[3,128]{1,0:T(4,128)S(1)}, u32[]{:S(2)}, u32[]{:S(2)}) %collective-permute-start.4) | collective-permute-done | bytes 1568 | tf_op jit(solution)/shard_map/ppermute | solution.py:76
  31.3 5.7 %collective-permute-done.5 = f32[3,128]{1,0:T(4,128)S(1)} collective-permute-done((f32[3,128]{1,0:T(4,128)S(1)}, f32[3,128]{1,0:T(4,128)S(1)}, u32[]{:S(2)}, u32[]{:S(2)}) %collective-permute-start.5) | collective-permute-done | bytes 1568 | tf_op jit(solution)/shard_map/ppermute | solution.py:76
  37.0 18.4 %all_gather.7 = f32[8,2048]{1,0:T(8,128)S(1)} all-gather(f32[8,128]{1,0:T(8,128)} %param.10), channel_id=1, replica_groups=mesh['group'=2,'src'=16] {'src'}, dimensions={1}, use_global_device_ids=true | all-gather | bytes 69632 | tf_op jit(solution)/shard_map/all_gather | solution.py:80
  55.6 18.5 %all_gather.6 = f32[3,2048]{1,0:T(4,128)S(1)} all-gather(f32[3,128]{1,0:T(4,128)S(1)} %pad_maximum_fusion.3), channel_id=1, replica_groups=mesh['group'=2,'src'=16] {'src'}, dimensions={1}, use_global_device_ids=true | all-gather | bytes 26112 | tf_op jit(solution)/shard_map/all_gather | solution.py:73
  74.5 0.8 pad_maximum_fusion.1
  75.2 4.6 %collective-permute-done.8 = f32[3,128]{1,0:T(4,128)S(1)} collective-permute-done((f32[3,128]{1,0:T(4,128)S(1)}, f32[3,128]{1,0:T(4,128)S(1)}, u32[]{:S(2)}, u32[]{:S(2)}) %collective-permute-start.8) | collective-permute-done | bytes 1568 | tf_op jit(solution)/shard_map/ppermute | solution.py:76
  79.8 5.7 %collective-permute-done.9 = f32[3,128]{1,0:T(4,128)S(1)} collective-permute-done((f32[3,128]{1,0:T(4,128)S(1)}, f32[3,128]{1,0:T(4,128)S(1)}, u32[]{:S(2)}, u32[]{:S(2)}) %collective-permute-start.9) | collective-permute-done | bytes 1568 | tf_op jit(solution)/shard_map/ppermute | solution.py:76
  87.1 4.1 %collective-permute-done.10 = f32[3,128]{1,0:T(4,128)S(1)} collective-permute-done((f32[3,128]{1,0:T(4,128)S(1)}, f32[3,128]{1,0:T(4,128)S(1)}, u32[]{:S(2)}, u32[]{:S(2)}) %collective-permute-start.10) | collective-permute-done | bytes 1568 | tf_op jit(solution)/shard_map/ppermute | solution.py:76
  91.2 0.8 fusion.15
  92.1 4.9 %collective-permute-done.11 = f32[3,128]{1,0:T(4,128)S(1)} collective-permute-done((f32[3,128]{1,0:T(4,128)S(1)}, f32[3,128]{1,0:T(4,128)S(1)}, u32[]{:S(2)}, u32[]{:S(2)}) %collective-permute-start.11) | collective-permute-done | bytes 1568 | tf_op jit(solution)/shard_map/ppermute | solution.py:76
  97.3 5.3 %collective-permute-done.12 = f32[3,128]{1,0:T(4,128)S(1)} collective-permute-done((f32[3,128]{1,0:T(4,128)S(1)}, f32[3,128]{1,0:T(4,128)S(1)}, u32[]{:S(2)}, u32[]{:S(2)}) %collective-permute-start.12) | collective-permute-done | bytes 1568 | tf_op jit(solution)/shard_map/ppermute | solution.py:76
  103.0 5.4 %collective-permute-done.13 = f32[3,128]{1,0:T(4,128)S(1)} collective-permute-done((f32[3,128]{1,0:T(4,128)S(1)}, f32[3,128]{1,0:T(4,128)S(1)}, u32[]{:S(2)}, u32[]{:S(2)}) %collective-permute-start.13) | collective-permute-done | bytes 1568 | tf_op jit(solution)/shard_map/ppermute | solution.py:76
  108.4 5.7 %collective-permute-done.14 = f32[3,128]{1,0:T(4,128)S(1)} collective-permute-done((f32[3,128]{1,0:T(4,128)S(1)}, f32[3,128]{1,0:T(4,128)S(1)}, u32[]{:S(2)}, u32[]{:S(2)}) %collective-permute-start.14) | collective-permute-done | bytes 1568 | tf_op jit(solution)/shard_map/ppermute | solution.py:76
  114.1 5.7 %collective-permute-done.15 = f32[3,128]{1,0:T(4,128)S(1)} collective-permute-done((f32[3,128]{1,0:T(4,128)S(1)}, f32[3,128]{1,0:T(4,128)S(1)}, u32[]{:S(2)}, u32[]{:S(2)}) %collective-permute-start.15) | collective-permute-done | bytes 1568 | tf_op jit(solution)/shard_map/ppermute | solution.py:76
  120.3 1.8 divide_multiply_fusion.1
  122.2 2.5 %multiply_reduce_fusion = (f32[3,128]{1,0:T(4,128)S(1)}, f32[128,2048]{1,0:T(8,128)S(1)}, f32[128,2048]{1,0:T(8,128)S(1)}, f32[128,2048]{1,0:T(8,128)S(1)}) fusion(f32[128,2048]{1,0:T(8,128)S(1)} %get-tuple-element.62, f32[128,2048]{1,0:T(8,128)S(1)} %get-tuple-element.92, f32[3,128]{1,0:T(4,128)S(1)} %bitcast.127, f32[128,2048]{1,0:T(8,128)S(1)} %get-tuple-element.94, ...), kind=kLoop, calls=%fused_computation.36 | loop fusion | flops 12582528 | bytes 8419328 | tf_op jit(solution)/shard_map/while/body/eval_jaxpr/transpose(jvp())/reduce_sum | solution.py:35
  125.6 2.0 %multiply_bitcast_fusion.5 = (f32[1,128,2048]{2,1,0:T(8,128)}, f32[128,2048]{1,0:T(8,128)}, f32[128,2048]{1,0:T(8,128)S(1)}) fusion(f32[3,128,2048]{2,1,0:T(8,128)S(1)} %get-tuple-element.98, f32[128,2048]{1,0:T(8,128)S(1)} %get-tuple-element.67, f32[128,2048]{1,0:T(8,128)S(1)} %get-tuple-element.54, f32[2048]{0:T(1024)S(1)} %broadcast_multiply_fusion.2, ...), kind=kLoop, calls=%fused_computation.57 | loop fusion | flops 2359296 | bytes 9445376 | tf_op jit(solution)/shard_map/while/body/eval_jaxpr/transpose(jvp())/broadcast_in_dim | solution.py:31
  127.6 2.3 %multiply_bitcast_fusion.3 = (f32[1,128,2048]{2,1,0:T(8,128)S(1)}, f32[128,2048]{1,0:T(8,128)}, f32[1,128,2048]{2,1,0:T(8,128)S(1)}, f32[128,2048]{1,0:T(8,128)}...) fusion(f32[3,128,2048]{2,1,0:T(8,128)S(1)} %get-tuple-element.98, f32[128,2048]{1,0:T(8,128)S(1)} %get-tuple-element.66, ...), kind=kLoop, calls=%fused_computation.55 | loop fusion | flops 5236736 | bytes 11575296 | tf_op jit(solution)/shard_map/while/body/eval_jaxpr/transpose(jvp())/broadcast_in_dim | solution.py:30
  129.8 4.8 %multiply_bitcast_fusion.11 = (f32[1,128,2048]{2,1,0:T(8,128)S(1)}, f32[1,128,2048]{2,1,0:T(8,128)S(1)}, f32[1,128,2048]{2,1,0:T(8,128)S(1)}, f32[1,128,2048]{2,...) fusion(f32[128,2048]{1,0:T(8,128)} %get-tuple-element.56, ...), kind=kLoop, calls=%fused_computation.65 | loop fusion | flops 3145728 | bytes 18874368 | tf_op jit(solution)/shard_map/while/body/eval_jaxpr/transpose(jvp())/broadcast_in_dim | solution.py:31
  134.6 3.4 %fusion.27 = (f32[3,128]{1,0:T(4,128)S(1)}, f32[3,2048]{1,0:T(4,128)S(1)}) fusion(f32[1,128,2048]{2,1,0:T(8,128)} %get-tuple-element.88, f32[1,128,2048]{2,1,0:T(8,128)S(1)} %get-tuple-element.70, f32[1,128,2048]{2,1,0:T(8,128)} %get-tuple-element.89, f32[1,128,2048]{2,1,0:T(8,128)S(1)} %get-tuple-element.58, f32[1,128,2048]{2,1,0:T(8,128)} %get-tuple-element.90, ...), kind=kLoop, calls=%fused_computation.144 | loop fusion | flops 11003520 | bytes 9490944 | tf_op jit(solution)/shard_map/while/body/eval_jaxpr/transpose(jvp())/reduce_sum | solution.py:26
  138.1 1.9 fusion.26
  140.2 1.0 scatter_custom_fusion
  141.2 1.2 scatter_fusion
  143.2 1.3 collective-permute-start.16
  144.6 0.7 collective-permute-done.16
  146.1 46.9 %reduce-scatter.2.cloned.1.call-done = f32[6,128]{1,0:T(8,128)} async-done(((f32[6,2048]{1,0:T(8,128)}), f32[6,128]{1,0:T(8,128)}) %reduce-scatter.2.cloned.1.call-update) | async-done | bytes 3088 | tf_op jit(solution)/shard_map/reduce_scatter | solution.py:99
  (96 shorter events, 7.2 us)
Async XLA Ops:
  7.2 185.8 %reduce-scatter.2.cloned.1.call-start = ((), (), s32[]{:S(2)}) async-start(), calls=%async_computation.1 | async-start | bytes 69632 | tf_op jit(solution)/shard_map/reduce_scatter | solution.py:99
  7.2 7.0 %collective-permute-start.1 = (f32[3,128]{1,0:T(4,128)}, f32[3,128]{1,0:T(4,128)S(1)}, u32[]{:S(2)}, u32[]{:S(2)}) collective-permute-start(f32[3,128]{1,0:T(4,128)} %param.9), channel_id=1, source_target_pairs={{0,1},{1,2},{2,3},{3,4},{4,5},{5,6},{6,7},{7,8},{8,9},{9,10},{10,1... | collective-permute-start | bytes 4616 | tf_op jit(solution)/shard_map/ppermute | solution.py:76
  7.7 66.7 %collective-permute-start = (f32[3,1]{1,0:T(4,128)}, f32[3,1]{1,0:T(4,128)S(1)}, u32[]{:S(2)}, u32[]{:S(2)}) collective-permute-start(f32[3,1]{1,0:T(4,128)} %bitcast.141), channel_id=1, source_target_pairs={{1,0},{2,1},{3,2},{4,3},{5,4},{6,5},{7,6},{8,7},{9,8},{10,9},{11,1... | collective-permute-start | bytes 44 | tf_op jit(solution)/shard_map/ppermute | solution.py:14
  14.2 5.7 %collective-permute-start.2 = (f32[3,128]{1,0:T(4,128)S(1)}, f32[3,128]{1,0:T(4,128)S(1)}, u32[]{:S(2)}, u32[]{:S(2)}) collective-permute-start(f32[3,128]{1,0:T(4,128)S(1)} %collective-permute-done.1), channel_id=1, source_target_pairs={{0,1},{1,2},{2,3},{3,4},{4,5},{5,6},{6,7},{7,8},{8,9},{9,10},{10,1... | collective-permute-start | bytes 4616 | tf_op jit(solution)/shard_map/ppermute | solution.py:76
  19.9 5.7 %collective-permute-start.3 = (f32[3,128]{1,0:T(4,128)S(1)}, f32[3,128]{1,0:T(4,128)S(1)}, u32[]{:S(2)}, u32[]{:S(2)}) collective-permute-start(f32[3,128]{1,0:T(4,128)S(1)} %collective-permute-done.2), channel_id=1, source_target_pairs={{0,1},{1,2},{2,3},{3,4},{4,5},{5,6},{6,7},{7,8},{8,9},{9,10},{10,1... | collective-permute-start | bytes 4616 | tf_op jit(solution)/shard_map/ppermute | solution.py:76
  25.6 5.7 %collective-permute-start.4 = (f32[3,128]{1,0:T(4,128)S(1)}, f32[3,128]{1,0:T(4,128)S(1)}, u32[]{:S(2)}, u32[]{:S(2)}) collective-permute-start(f32[3,128]{1,0:T(4,128)S(1)} %collective-permute-done.3), channel_id=1, source_target_pairs={{0,1},{1,2},{2,3},{3,4},{4,5},{5,6},{6,7},{7,8},{8,9},{9,10},{10,1... | collective-permute-start | bytes 4616 | tf_op jit(solution)/shard_map/ppermute | solution.py:76
  31.3 5.7 %collective-permute-start.5 = (f32[3,128]{1,0:T(4,128)S(1)}, f32[3,128]{1,0:T(4,128)S(1)}, u32[]{:S(2)}, u32[]{:S(2)}) collective-permute-start(f32[3,128]{1,0:T(4,128)S(1)} %collective-permute-done.4), channel_id=1, source_target_pairs={{0,1},{1,2},{2,3},{3,4},{4,5},{5,6},{6,7},{7,8},{8,9},{9,10},{10,1... | collective-permute-start | bytes 4616 | tf_op jit(solution)/shard_map/ppermute | solution.py:76
  37.0 18.4 %collective-permute-start.6 = (f32[3,128]{1,0:T(4,128)S(1)}, f32[3,128]{1,0:T(4,128)S(1)}, u32[]{:S(2)}, u32[]{:S(2)}) collective-permute-start(f32[3,128]{1,0:T(4,128)S(1)} %collective-permute-done.5), channel_id=1, source_target_pairs={{0,1},{1,2},{2,3},{3,4},{4,5},{5,6},{6,7},{7,8},{8,9},{9,10},{10,1... | collective-permute-start | bytes 4616 | tf_op jit(solution)/shard_map/ppermute | solution.py:76
  55.4 18.7 %collective-permute-start.7 = (f32[3,128]{1,0:T(4,128)S(1)}, f32[3,128]{1,0:T(4,128)S(1)}, u32[]{:S(2)}, u32[]{:S(2)}) collective-permute-start(f32[3,128]{1,0:T(4,128)S(1)} %collective-permute-done.6), channel_id=1, source_target_pairs={{0,1},{1,2},{2,3},{3,4},{4,5},{5,6},{6,7},{7,8},{8,9},{9,10},{10,1... | collective-permute-start | bytes 4616 | tf_op jit(solution)/shard_map/ppermute | solution.py:76
  74.1 5.7 %collective-permute-start.8 = (f32[3,128]{1,0:T(4,128)S(1)}, f32[3,128]{1,0:T(4,128)S(1)}, u32[]{:S(2)}, u32[]{:S(2)}) collective-permute-start(f32[3,128]{1,0:T(4,128)S(1)} %collective-permute-done.7), channel_id=1, source_target_pairs={{0,1},{1,2},{2,3},{3,4},{4,5},{5,6},{6,7},{7,8},{8,9},{9,10},{10,1... | collective-permute-start | bytes 4616 | tf_op jit(solution)/shard_map/ppermute | solution.py:76
  79.8 5.7 %collective-permute-start.9 = (f32[3,128]{1,0:T(4,128)S(1)}, f32[3,128]{1,0:T(4,128)S(1)}, u32[]{:S(2)}, u32[]{:S(2)}) collective-permute-start(f32[3,128]{1,0:T(4,128)S(1)} %collective-permute-done.8), channel_id=1, source_target_pairs={{0,1},{1,2},{2,3},{3,4},{4,5},{5,6},{6,7},{7,8},{8,9},{9,10},{10,1... | collective-permute-start | bytes 4616 | tf_op jit(solution)/shard_map/ppermute | solution.py:76
  85.5 5.7 %collective-permute-start.10 = (f32[3,128]{1,0:T(4,128)S(1)}, f32[3,128]{1,0:T(4,128)S(1)}, u32[]{:S(2)}, u32[]{:S(2)}) collective-permute-start(f32[3,128]{1,0:T(4,128)S(1)} %collective-permute-done.9), channel_id=1, source_target_pairs={{0,1},{1,2},{2,3},{3,4},{4,5},{5,6},{6,7},{7,8},{8,9},{9,10},{10,1... | collective-permute-start | bytes 4616 | tf_op jit(solution)/shard_map/ppermute | solution.py:76
  91.2 5.7 %collective-permute-start.11 = (f32[3,128]{1,0:T(4,128)S(1)}, f32[3,128]{1,0:T(4,128)S(1)}, u32[]{:S(2)}, u32[]{:S(2)}) collective-permute-start(f32[3,128]{1,0:T(4,128)S(1)} %collective-permute-done.10), channel_id=1, source_target_pairs={{0,1},{1,2},{2,3},{3,4},{4,5},{5,6},{6,7},{7,8},{8,9},{9,10},{10,1... | collective-permute-start | bytes 4616 | tf_op jit(solution)/shard_map/ppermute | solution.py:76
  96.9 5.7 %collective-permute-start.12 = (f32[3,128]{1,0:T(4,128)S(1)}, f32[3,128]{1,0:T(4,128)S(1)}, u32[]{:S(2)}, u32[]{:S(2)}) collective-permute-start(f32[3,128]{1,0:T(4,128)S(1)} %collective-permute-done.11), channel_id=1, source_target_pairs={{0,1},{1,2},{2,3},{3,4},{4,5},{5,6},{6,7},{7,8},{8,9},{9,10},{10,1... | collective-permute-start | bytes 4616 | tf_op jit(solution)/shard_map/ppermute | solution.py:76
  97.0 23.0 %copy-start.1 = (f32[3,128]{1,0:T(4,128)S(1)}, f32[3,128]{1,0:T(4,128)}, u32[]{:S(2)}) copy-start(f32[3,128]{1,0:T(4,128)} %param.9) | copy-start | bytes 4612
  97.0 23.3 %copy-start.3 = (f32[8,128]{1,0:T(8,128)S(1)}, f32[8,128]{1,0:T(8,128)}, u32[]{:S(2)}) copy-start(f32[8,128]{1,0:T(8,128)} %param.13) | copy-start | bytes 12292
  97.0 23.3 %copy-start.4 = (f32[8]{0:T(128)S(1)}, f32[8]{0:T(128)}, u32[]{:S(2)}) copy-start(f32[8]{0:T(128)} %param.14) | copy-start | bytes 100
  102.7 5.7 %collective-permute-start.13 = (f32[3,128]{1,0:T(4,128)S(1)}, f32[3,128]{1,0:T(4,128)S(1)}, u32[]{:S(2)}, u32[]{:S(2)}) collective-permute-start(f32[3,128]{1,0:T(4,128)S(1)} %collective-permute-done.12), channel_id=1, source_target_pairs={{0,1},{1,2},{2,3},{3,4},{4,5},{5,6},{6,7},{7,8},{8,9},{9,10},{10,1... | collective-permute-start | bytes 4616 | tf_op jit(solution)/shard_map/ppermute | solution.py:76
  108.4 5.7 %collective-permute-start.14 = (f32[3,128]{1,0:T(4,128)S(1)}, f32[3,128]{1,0:T(4,128)S(1)}, u32[]{:S(2)}, u32[]{:S(2)}) collective-permute-start(f32[3,128]{1,0:T(4,128)S(1)} %collective-permute-done.13), channel_id=1, source_target_pairs={{0,1},{1,2},{2,3},{3,4},{4,5},{5,6},{6,7},{7,8},{8,9},{9,10},{10,1... | collective-permute-start | bytes 4616 | tf_op jit(solution)/shard_map/ppermute | solution.py:76
  114.1 5.7 %collective-permute-start.15 = (f32[3,128]{1,0:T(4,128)S(1)}, f32[3,128]{1,0:T(4,128)S(1)}, u32[]{:S(2)}, u32[]{:S(2)}) collective-permute-start(f32[3,128]{1,0:T(4,128)S(1)} %collective-permute-done.14), channel_id=1, source_target_pairs={{0,1},{1,2},{2,3},{3,4},{4,5},{5,6},{6,7},{7,8},{8,9},{9,10},{10,1... | collective-permute-start | bytes 4616 | tf_op jit(solution)/shard_map/ppermute | solution.py:76
  134.6 3.4 %copy-start = (f32[1,128,2048]{2,1,0:T(8,128)S(1)}, f32[1,128,2048]{2,1,0:T(8,128)}, u32[]{:S(2)}) copy-start(f32[1,128,2048]{2,1,0:T(8,128)} %get-tuple-element.87) | copy-start | bytes 3145732
  138.0 4.4 %copy-start.2 = (f32[3]{0:T(128)S(1)}, f32[3]{0:T(128)}, u32[]{:S(2)}) copy-start(f32[3]{0:T(128)} %constant.73.clone) | copy-start | bytes 40
  143.2 2.1 %collective-permute-start.16 = (f32[3,1]{0,1:T(1,128)S(1)}, f32[3,1]{0,1:T(1,128)S(1)}, u32[]{:S(2)}, u32[]{:S(2)}) collective-permute-start(f32[3,1]{0,1:T(1,128)S(1)} %slice.105), channel_id=1, source_target_pairs={{0,1},{1,2},{2,3},{3,4},{4,5},{5,6},{6,7},{7,8},{8,9},{9,10},{10,1... | collective-permute-start | bytes 44 | tf_op jit(solution)/shard_map/ppermute | solution.py:14
Sparse Core Ops, SparseCore 0:
  143.3 49.6 reduce-scatter.1
